TPU v7x, 256 devices: a whole 4x4x8 slice. The times are simulated.
256 devices in a mesh: dp: 128 (over y, z, x), tensor: 2 (over core).
Axes of the slice: x: 4, y: 4, z: 8, core: 2. Of those that a mesh axis runs over, the one named last changes fastest.
Arguments:
- fc_grads: bfloat16 [128, 768, 3072], P('dp', None, 'tensor')
- fc_error: bfloat16 [128, 768, 3072], P('dp', None, 'tensor'), may hold values from -4 to 4
- query: float32 [3072, 32], P('tensor'), may hold values from -0.109375 to 0.109375
- gram_inverse: float32 [32, 32], replicated
- fc_master: float32 [768, 3072], P('dp', 'tensor'), may hold values from -6 to 6
- fc_momentum: float32 [768, 3072], P('dp', 'tensor'), may hold values from -3 to 3
- vec_grads: bfloat16 [128, 5376], P('dp'), may hold values from -24 to 24
- vec_master: float32 [5376], P('dp'), may hold values from -6 to 6
- vec_momentum: float32 [5376], P('dp'), may hold values from -4 to 4
Outputs:
- new_error: bfloat16 [128, 768, 3072], P('dp', None, 'tensor')
- new_momentum: float32 [768, 3072], P('dp', 'tensor')
- new_master: float32 [768, 3072], P('dp', 'tensor')
- new_weights: bfloat16 [768, 3072], P(None, 'tensor')
- vec_new_momentum: float32 [5376], P('dp')
- vec_new_master: float32 [5376], P('dp')
- vec_weights: bfloat16 [5376], replicated
All inputs are finite; a program needn't handle non-finite values.
Results may differ from a plain program's by a relative error of at most 0.0085.
Values may be sent and summed in bfloat16 or wider, within the bound.
No kernel may reach another device: no remote copies, remote signals or barrier semaphores. Data moves between devices by JAX's collectives and lax.ppermute only.
A program may use at most 64 MiB of HBM per device.

v0:
```python
import jax
import jax.numpy as jnp
from jax import lax
from jax.sharding import PartitionSpec as P

momentum_decay = 0.9
step_size = 0.5


def on_device(
    fc_grads,
    fc_error,
    query,
    gram_inverse,
    fc_master,
    fc_momentum,
    vec_grads,
    vec_master,
    vec_momentum,
):
    replicas = lax.axis_size("dp")
    replica_index = lax.axis_index("dp")
    merged = (fc_grads[0].astype(jnp.float32) + fc_error[0].astype(jnp.float32)).astype(
        jnp.bfloat16
    )
    query_b = query.astype(jnp.bfloat16)
    row_part = jnp.dot(merged, query_b, preferred_element_type=jnp.float32)
    vec_term = vec_grads[0].astype(jnp.float32)
    shard_len = vec_master.shape[0]
    row_total = lax.psum(row_part, ("dp", "tensor"))
    vec_total = lax.psum(vec_term, "dp")
    vec_mean = (
        lax.dynamic_slice_in_dim(vec_total, replica_index * shard_len, shard_len, 0) / replicas
    )
    row_mean = row_total / replicas
    row_basis = jnp.dot(row_mean, gram_inverse, precision=lax.Precision.HIGHEST)
    basis_b = row_basis.astype(jnp.bfloat16)
    col_part = lax.dot_general(
        merged, basis_b, (((0,), (0,)), ((), ())), preferred_element_type=jnp.float32
    )
    col_mean = lax.psum(col_part, "dp") / replicas
    approx = jnp.dot(row_basis, col_mean.T, precision=lax.Precision.HIGHEST)
    new_error = (merged.astype(jnp.float32) - approx).astype(jnp.bfloat16)[None]
    state_rows = fc_master.shape[0]
    basis_rows = lax.dynamic_slice_in_dim(row_basis, replica_index * state_rows, state_rows, 0)
    approx_rows = jnp.dot(basis_rows, col_mean.T, precision=lax.Precision.HIGHEST)
    new_momentum = momentum_decay * fc_momentum + approx_rows
    new_master = fc_master - step_size * (approx_rows + momentum_decay * new_momentum)
    vec_new_momentum = momentum_decay * vec_momentum + vec_mean
    vec_new_master = vec_master - step_size * (vec_mean + momentum_decay * vec_new_momentum)
    new_weights, vec_weights = (
        lax.all_gather(new_master.astype(jnp.bfloat16), "dp", axis=0, tiled=True),
        lax.all_gather(vec_new_master.astype(jnp.bfloat16), "dp", axis=0, tiled=True),
    )
    return (
        new_error,
        new_momentum,
        new_master,
        new_weights,
        vec_new_momentum,
        vec_new_master,
        vec_weights,
    )


def solution(mesh):
    return jax.shard_map(
        on_device,
        mesh=mesh,
        in_specs=(
            P("dp", None, "tensor"),
            P("dp", None, "tensor"),
            P("tensor", None),
            P(),
            P("dp", "tensor"),
            P("dp", "tensor"),
            P("dp", None),
            P("dp"),
            P("dp"),
        ),
        out_specs=(
            P("dp", None, "tensor"),
            P("dp", "tensor"),
            P("dp", "tensor"),
            P(None, "tensor"),
            P("dp"),
            P("dp"),
            P(),
        ),
        check_vma=False,
    )
```

profile of v0, /device:TPU:0, one launch (start us, length us, event | category | flops | bytes accessed | tf_op | source)
XLA Modules:
  0.0 1860.5 jit_solution(18031364214805871848)
XLA Ops:
  7.2 0.0 copy-start
  7.2 0.0 copy-start.1
  7.2 0.0 all-reduce.4.cloned.1.call-start
  7.2 4.0 fusion.9
  11.2 0.0 all-reduce.4.cloned.1.call-update
  11.2 0.0 all-reduce.6.cloned.1.call-start
  11.3 244.5 %all-reduce.4.cloned.1.call-done = f32[768,32]{0,1:T(8,128)} async-done(((f32[768,32]{0,1:T(8,128)}), f32[768,32]{0,1:T(8,128)}) %all-reduce.4.cloned.1.call-update) | async-done | bytes 98320 | tf_op jit(solution)/shard_map/psum | solution.py:30
  255.8 0.0 copy-done
  255.8 1.2 fusion.7
  256.9 0.0 copy-done.1
  256.9 0.0 copy-start.2
  257.0 0.0 copy-start.3
  257.0 0.0 copy-start.7
  257.0 0.0 copy-start.4
  257.0 0.0 copy-start.5
  257.0 0.0 copy-start.6
  257.0 3.1 fusion.11
  260.1 0.0 all-reduce.6.cloned.1.call-update
  260.1 0.0 all-gather.3.cloned.1.call-start
  260.2 209.9 %all-reduce.6.cloned.1.call-done = f32[1536,32]{0,1:T(8,128)} async-done(((f32[1536,32]{0,1:T(8,128)}), f32[1536,32]{0,1:T(8,128)}) %all-reduce.6.cloned.1.call-update) | async-done | bytes 196624 | tf_op jit(solution)/shard_map/psum | solution.py:41
  470.1 0.0 copy-done.2
  470.1 0.0 copy-done.3
  470.1 1.9 convert_bitcast_fusion
  472.0 0.0 all-gather.3.cloned.1.call-update
  472.0 0.0 copy-done.7
  472.0 0.6 dynamic-slice
  473.3 0.0 copy-done.4
  473.3 0.1 convert_reduce_fusion
  473.4 686.4 %psum.23 = f32[5376]{0:T(1024)S(1)} all-reduce(f32[5376]{0:T(1024)S(1)} %convert_reduce_fusion), channel_id=1, replica_groups=mesh['dp'=128,'tensor'=2] {'dp'}, use_global_device_ids=true, to_apply=%region_2.0 | all-reduce | flops 5376 | bytes 43008 | tf_op jit(solution)/shard_map/psum | solution.py:31
  1159.7 0.0 copy-done.5
  1159.7 0.0 copy-done.6
  1159.7 0.6 fusion.21
  1160.3 0.2 dynamic-update-slice
  1160.5 681.7 %all-reduce = bf16[5376]{0:T(1024)(128)(2,1)} all-reduce(bf16[5376]{0:T(1024)(128)(2,1)S(1)} %dynamic-update-slice), channel_id=1, replica_groups=mesh['dp'=128,'tensor'=2] {'dp'}, use_global_device_ids=true, to_apply=%add | all-reduce | flops 5376 | bytes 21504
  1842.3 6.6 fusion
  1848.9 0.0 all-gather.3.cloned.1.call-done
  1848.9 5.0 reshape.25
  (1 shorter events, 0.0 us)
Async XLA Ops:
  7.2 248.6 %copy-start = (f32[32,32]{1,0:T(8,128)S(1)}, f32[32,32]{1,0:T(8,128)}, u32[]{:S(2)}) copy-start(f32[32,32]{1,0:T(8,128)} %param.12) | copy-start | bytes 12292
  7.2 249.8 %copy-start.1 = (bf16[1,768,1536]{2,1,0:T(8,128)(2,1)S(1)}, bf16[1,768,1536]{2,1,0:T(8,128)(2,1)}, u32[]{:S(2)}) copy-start(bf16[1,768,1536]{2,1,0:T(8,128)(2,1)} %param.10) | copy-start | bytes 7077892
  7.2 248.6 %all-reduce.4.cloned.1.call-start = ((), (), s32[]{:S(2)}) async-start(), calls=%async_computation | async-start | bytes 196608 | tf_op jit(solution)/shard_map/psum | solution.py:30
  11.2 458.9 %all-reduce.6.cloned.1.call-start = ((), (), s32[]{:S(2)}) async-start(), calls=%async_computation.1 | async-start | bytes 393216 | tf_op jit(solution)/shard_map/psum | solution.py:41
  256.9 213.1 %copy-start.2 = (f32[6,1536]{1,0:T(8,128)S(1)}, f32[6,1536]{1,0:T(8,128)}, u32[]{:S(2)}) copy-start(f32[6,1536]{1,0:T(8,128)} %param.13) | copy-start | bytes 110596
  257.0 213.1 %copy-start.3 = (f32[6,1536]{1,0:T(8,128)S(1)}, f32[6,1536]{1,0:T(8,128)}, u32[]{:S(2)}) copy-start(f32[6,1536]{1,0:T(8,128)} %param.14) | copy-start | bytes 110596
  257.0 215.1 %copy-start.7 = (u32[256]{0:T(256)S(1)}, u32[256]{0:T(256)}, u32[]{:S(2)}) copy-start(u32[256]{0:T(256)} %constant.38) | copy-start | bytes 3076
  257.0 216.3 %copy-start.4 = (bf16[1,5376]{1,0:T(2,128)(2,1)S(1)}, bf16[1,5376]{1,0:T(2,128)(2,1)}, u32[]{:S(2)}) copy-start(bf16[1,5376]{1,0:T(2,128)(2,1)} %param.15) | copy-start | bytes 32260
  257.0 902.7 %copy-start.5 = (f32[42]{0:T(128)S(1)}, f32[42]{0:T(128)}, u32[]{:S(2)}) copy-start(f32[42]{0:T(128)} %param.16) | copy-start | bytes 508
  257.0 902.7 %copy-start.6 = (f32[42]{0:T(128)S(1)}, f32[42]{0:T(128)}, u32[]{:S(2)}) copy-start(f32[42]{0:T(128)} %param.17) | copy-start | bytes 508
  260.1 1588.8 %all-gather.3.cloned.1.call-start = ((), (), s32[]{:S(2)}) async-start(), calls=%async_computation.2 | async-start | bytes 3170304 | tf_op jit(solution)/shard_map/all_gather | solution.py:52
Sparse Core Ops, SparseCore 0:
  14.1 241.6 all-reduce.3
  261.8 208.2 all-reduce.5
  475.0 112.6 all-gather.2
where the time goes:
time: 1860 us
  blocking collectives  1370 us (74%)
  waiting for transfers between devices  454 us (24%)
    psum x1, blocking collectives, on_device(): vec_total = lax.psum(vec_term, 'dp')  686 us
    unnamed x1, blocking collectives  682 us
    psum x1, waiting for transfers between devices, on_device(): row_total = lax.psum(row_part, ('dp', 'tensor'))  244 us
    psum x1, waiting for transfers between devices, on_device(): col_mean = lax.psum(col_part, 'dp') / replicas  210 us
  transfers between devices with their start and end apart: 3, of which 2 were waited for; matrix products, arithmetic and copies ran while one was open for 0% of the time, Pallas kernels for 0%

commit v1 on v0

--- a/solution.py
+++ b/solution.py
@@ -27,7 +27,8 @@
     row_part = jnp.dot(merged, query_b, preferred_element_type=jnp.float32)
     vec_term = vec_grads[0].astype(jnp.float32)
     shard_len = vec_master.shape[0]
-    row_total = lax.psum(row_part, ("dp", "tensor"))
+    terms = lax.all_gather(row_part, ("dp", "tensor"))
+    row_total = jnp.sum(terms, axis=0)
     vec_total = lax.psum(vec_term, "dp")
     vec_mean = (
         lax.dynamic_slice_in_dim(vec_total, replica_index * shard_len, shard_len, 0) / replicas

time: 1860 us -> 1770 us (0.952)
  waiting for transfers between devices: 454 us -> 349 us
    psum x1 -> x0, waiting for transfers between devices: 244 us -> none  [on_device(): row_total = lax.psum(row_part, ('dp', 'tensor'))]
    all_gather x0 -> x1, waiting for transfers between devices: none -> 140 us  [on_device(): terms = lax.all_gather(row_part, ('dp', 'tensor'))]
where the time goes in v1:
time: 1770 us
  blocking collectives  1370 us (77%)
  waiting for transfers between devices  349 us (20%)
  local copies, waits for them, and re-layouts  21.1 us (1%)
    psum x1, blocking collectives, on_device(): vec_total = lax.psum(vec_term, 'dp')  686 us
    unnamed x1, blocking collectives  682 us
    psum x1, waiting for transfers between devices, on_device(): col_mean = lax.psum(col_part, 'dp') / replicas  209 us
    all_gather x1, waiting for transfers between devices, on_device(): terms = lax.all_gather(row_part, ('dp', 'tensor'))  140 us
  transfers between devices with their start and end apart: 3, of which 2 were waited for; matrix products, arithmetic and copies ran while one was open for 0% of the time, Pallas kernels for 0%

profile of v1, /device:TPU:0, one launch (start us, length us, event | category | flops | bytes accessed | tf_op | source)
XLA Modules:
  0.0 1770.9 jit_solution(14410806995569889100)
XLA Ops:
  7.2 0.0 copy-start
  7.2 0.0 all-gather.5.cloned.1.call-start
  7.2 3.8 fusion.9
  11.0 0.0 all-gather.5.cloned.1.call-update
  11.1 0.0 all-reduce.3.cloned.1.call-start
  11.1 140.1 %all-gather.5.cloned.1.call-done = f32[196608,32]{0,1:T(8,128)} async-done(((f32[768,32]{0,1:T(8,128)}), f32[196608,32]{0,1:T(8,128)}) %all-gather.5.cloned.1.call-update) | async-done | bytes 25165840 | tf_op jit(solution)/shard_map/all_gather | solution.py:30
  151.2 15.2 copy.16
  166.5 0.0 copy-start.1
  166.5 0.0 copy-start.2
  166.5 3.3 bitcast_reduce_fusion
  169.8 0.0 copy-done
  169.8 0.3 fusion.7
  170.1 0.0 copy-done.1
  170.1 0.0 copy-done.2
  170.1 0.0 copy-start.3
  170.2 0.0 copy-start.4
  170.2 0.0 copy-start.8
  170.2 0.0 copy-start.5
  170.2 0.0 copy-start.6
  170.2 0.0 copy-start.7
  170.2 1.4 fusion.11
  171.7 0.0 all-reduce.3.cloned.1.call-update
  171.7 0.0 all-gather.7.cloned.1.call-start
  171.7 208.8 %all-reduce.3.cloned.1.call-done = f32[1536,32]{0,1:T(8,128)} async-done(((f32[1536,32]{0,1:T(8,128)}), f32[1536,32]{0,1:T(8,128)}) %all-reduce.3.cloned.1.call-update) | async-done | bytes 196624 | tf_op jit(solution)/shard_map/psum | solution.py:42
  380.6 0.0 copy-done.3
  380.6 0.0 copy-done.4
  380.6 1.9 convert_bitcast_fusion
  382.5 0.0 all-gather.7.cloned.1.call-update
  382.5 0.0 copy-done.8
  382.5 0.6 dynamic-slice
  383.8 0.0 copy-done.5
  383.8 0.1 convert_reduce_fusion
  383.8 686.4 %psum.15 = f32[5376]{0:T(1024)S(1)} all-reduce(f32[5376]{0:T(1024)S(1)} %convert_reduce_fusion), channel_id=1, replica_groups=mesh['dp'=128,'tensor'=2] {'dp'}, use_global_device_ids=true, to_apply=%region_2.0 | all-reduce | flops 5376 | bytes 43008 | tf_op jit(solution)/shard_map/psum | solution.py:32
  1070.2 0.0 copy-done.6
  1070.2 0.0 copy-done.7
  1070.2 0.6 fusion.21
  1070.8 0.2 dynamic-update-slice
  1071.0 681.7 %all-reduce = bf16[5376]{0:T(1024)(128)(2,1)} all-reduce(bf16[5376]{0:T(1024)(128)(2,1)S(1)} %dynamic-update-slice), channel_id=1, replica_groups=mesh['dp'=128,'tensor'=2] {'dp'}, use_global_device_ids=true, to_apply=%add | all-reduce | flops 5376 | bytes 21504
  1752.8 6.6 fusion
  1759.4 0.0 all-gather.7.cloned.1.call-done
  1759.4 5.0 reshape.26
  (1 shorter events, 0.0 us)
Async XLA Ops:
  7.2 162.7 %copy-start = (f32[32,32]{1,0:T(8,128)S(1)}, f32[32,32]{1,0:T(8,128)}, u32[]{:S(2)}) copy-start(f32[32,32]{1,0:T(8,128)} %param.12) | copy-start | bytes 12292
  7.2 144.1 %all-gather.5.cloned.1.call-start = ((), (), s32[]{:S(2)}) async-start(), calls=%async_computation.1 | async-start | bytes 25264128 | tf_op jit(solution)/shard_map/all_gather | solution.py:30
  11.1 369.5 %all-reduce.3.cloned.1.call-start = ((), (), s32[]{:S(2)}) async-start(), calls=%async_computation | async-start | bytes 393216 | tf_op jit(solution)/shard_map/psum | solution.py:42
  166.5 3.6 copy-start.1
  166.5 3.6 copy-start.2
  170.1 210.4 %copy-start.3 = (f32[6,1536]{1,0:T(8,128)S(1)}, f32[6,1536]{1,0:T(8,128)}, u32[]{:S(2)}) copy-start(f32[6,1536]{1,0:T(8,128)} %param.13) | copy-start | bytes 110596
  170.2 210.4 %copy-start.4 = (f32[6,1536]{1,0:T(8,128)S(1)}, f32[6,1536]{1,0:T(8,128)}, u32[]{:S(2)}) copy-start(f32[6,1536]{1,0:T(8,128)} %param.14) | copy-start | bytes 110596
  170.2 212.3 %copy-start.8 = (u32[256]{0:T(256)S(1)}, u32[256]{0:T(256)}, u32[]{:S(2)}) copy-start(u32[256]{0:T(256)} %constant.40) | copy-start | bytes 3076
  170.2 213.6 %copy-start.5 = (bf16[1,5376]{1,0:T(2,128)(2,1)S(1)}, bf16[1,5376]{1,0:T(2,128)(2,1)}, u32[]{:S(2)}) copy-start(bf16[1,5376]{1,0:T(2,128)(2,1)} %param.15) | copy-start | bytes 32260
  170.2 900.0 %copy-start.6 = (f32[42]{0:T(128)S(1)}, f32[42]{0:T(128)}, u32[]{:S(2)}) copy-start(f32[42]{0:T(128)} %param.16) | copy-start | bytes 508
  170.2 900.0 %copy-start.7 = (f32[42]{0:T(128)S(1)}, f32[42]{0:T(128)}, u32[]{:S(2)}) copy-start(f32[42]{0:T(128)} %param.17) | copy-start | bytes 508
  171.7 1587.7 %all-gather.7.cloned.1.call-start = ((), (), s32[]{:S(2)}) async-start(), calls=%async_computation.2 | async-start | bytes 3170304 | tf_op jit(solution)/shard_map/all_gather | solution.py:53
Sparse Core Ops, SparseCore 0:
  12.3 138.8 all-gather.4
  171.8 208.7 all-reduce.2
  385.4 112.6 all-gather.6

commit v2 on v0

--- a/solution.py
+++ b/solution.py
@@ -27,7 +27,8 @@
     row_part = jnp.dot(merged, query_b, preferred_element_type=jnp.float32)
     vec_term = vec_grads[0].astype(jnp.float32)
     shard_len = vec_master.shape[0]
-    row_total = lax.psum(row_part, ("dp", "tensor"))
+    partial = lax.psum(row_part, "tensor")
+    row_total = lax.psum(partial, "dp")
     vec_total = lax.psum(vec_term, "dp")
     vec_mean = (
         lax.dynamic_slice_in_dim(vec_total, replica_index * shard_len, shard_len, 0) / replicas

time: 1860 us -> 1870 us (level)
    psum x1 -> x2, waiting for transfers between devices: 244 us -> 247 us  [the longest x1 217 us: on_device(): row_total = lax.psum(partial, 'dp')]
  transfers between devices with their start and end apart: 3 -> 4, of which waited for: 2 -> 3; matrix products, arithmetic and copies ran while one was open for 0% -> 0% of each run, Pallas kernels for 0% -> 0%
where the time goes in v2:
time: 1870 us
  blocking collectives  1370 us (73%)
  waiting for transfers between devices  459 us (25%)
    psum x1, blocking collectives, on_device(): vec_total = lax.psum(vec_term, 'dp')  686 us
    unnamed x1, blocking collectives  682 us
    psum x1, waiting for transfers between devices, on_device(): row_total = lax.psum(partial, 'dp')  217 us
    psum x1, waiting for transfers between devices, on_device(): col_mean = lax.psum(col_part, 'dp') / replicas  212 us
  transfers between devices with their start and end apart: 4, of which 3 were waited for; matrix products, arithmetic and copies ran while one was open for 0% of the time, Pallas kernels for 0%

profile of v2, /device:TPU:0, one launch (start us, length us, event | category | flops | bytes accessed | tf_op | source)
XLA Modules:
  0.0 1865.1 jit_solution(8462455478323851707)
XLA Ops:
  7.2 0.0 copy-start
  7.2 0.0 copy-start.1
  7.2 0.0 all-reduce.5.cloned.1.call-start
  7.2 4.0 fusion.9
  11.2 0.0 all-reduce.5.cloned.1.call-update
  11.2 0.0 all-reduce.7.cloned.1.call-start
  11.3 30.2 %all-reduce.5.cloned.1.call-done = f32[768,32]{0,1:T(8,128)} async-done(((f32[768,32]{0,1:T(8,128)}), f32[768,32]{0,1:T(8,128)}) %all-reduce.5.cloned.1.call-update) | async-done | bytes 98320 | tf_op jit(solution)/shard_map/psum | solution.py:30
  41.5 0.0 all-reduce.7.cloned.1.call-update
  41.5 0.0 all-reduce.9.cloned.1.call-start
  41.6 216.7 %all-reduce.7.cloned.1.call-done = f32[768,32]{0,1:T(8,128)} async-done(((f32[768,32]{0,1:T(8,128)}), f32[768,32]{0,1:T(8,128)}) %all-reduce.7.cloned.1.call-update) | async-done | bytes 98320 | tf_op jit(solution)/shard_map/psum | solution.py:31
  258.3 0.0 copy-done
  258.3 1.2 fusion.7
  259.5 0.0 copy-done.1
  259.5 0.0 copy-start.2
  259.5 0.0 copy-start.3
  259.5 0.0 copy-start.7
  259.5 0.0 copy-start.4
  259.5 0.0 copy-start.5
  259.5 0.0 copy-start.6
  259.5 3.1 fusion.11
  262.7 0.0 all-reduce.9.cloned.1.call-update
  262.7 0.0 all-gather.3.cloned.1.call-start
  262.7 212.0 %all-reduce.9.cloned.1.call-done = f32[1536,32]{0,1:T(8,128)} async-done(((f32[1536,32]{0,1:T(8,128)}), f32[1536,32]{0,1:T(8,128)}) %all-reduce.9.cloned.1.call-update) | async-done | bytes 196624 | tf_op jit(solution)/shard_map/psum | solution.py:42
  474.7 0.0 copy-done.2
  474.7 0.0 copy-done.3
  474.7 1.9 convert_bitcast_fusion
  476.6 0.0 all-gather.3.cloned.1.call-update
  476.7 0.0 copy-done.7
  476.7 0.6 dynamic-slice
  477.9 0.0 copy-done.4
  477.9 0.1 convert_reduce_fusion
  478.0 686.3 %psum.31 = f32[5376]{0:T(1024)S(1)} all-reduce(f32[5376]{0:T(1024)S(1)} %convert_reduce_fusion), channel_id=1, replica_groups=mesh['dp'=128,'tensor'=2] {'dp'}, use_global_device_ids=true, to_apply=%region_3.0 | all-reduce | flops 5376 | bytes 43008 | tf_op jit(solution)/shard_map/psum | solution.py:32
  1164.3 0.0 copy-done.5
  1164.3 0.0 copy-done.6
  1164.3 0.6 fusion.21
  1164.9 0.2 dynamic-update-slice
  1165.1 681.7 %all-reduce = bf16[5376]{0:T(1024)(128)(2,1)} all-reduce(bf16[5376]{0:T(1024)(128)(2,1)S(1)} %dynamic-update-slice), channel_id=1, replica_groups=mesh['dp'=128,'tensor'=2] {'dp'}, use_global_device_ids=true, to_apply=%add | all-reduce | flops 5376 | bytes 21504
  1846.9 6.6 fusion
  1853.5 0.0 all-gather.3.cloned.1.call-done
  1853.5 5.0 reshape.25
  (1 shorter events, 0.0 us)
Async XLA Ops:
  7.2 251.1 %copy-start = (f32[32,32]{1,0:T(8,128)S(1)}, f32[32,32]{1,0:T(8,128)}, u32[]{:S(2)}) copy-start(f32[32,32]{1,0:T(8,128)} %param.12) | copy-start | bytes 12292
  7.2 252.3 %copy-start.1 = (bf16[1,768,1536]{2,1,0:T(8,128)(2,1)S(1)}, bf16[1,768,1536]{2,1,0:T(8,128)(2,1)}, u32[]{:S(2)}) copy-start(bf16[1,768,1536]{2,1,0:T(8,128)(2,1)} %param.10) | copy-start | bytes 7077892
  7.2 34.3 %all-reduce.5.cloned.1.call-start = ((), (), s32[]{:S(2)}) async-start(), calls=%async_computation | async-start | bytes 196608 | tf_op jit(solution)/shard_map/psum | solution.py:30
  11.2 247.1 %all-reduce.7.cloned.1.call-start = ((), (), s32[]{:S(2)}) async-start(), calls=%async_computation.1 | async-start | bytes 196608 | tf_op jit(solution)/shard_map/psum | solution.py:31
  41.5 433.2 %all-reduce.9.cloned.1.call-start = ((), (), s32[]{:S(2)}) async-start(), calls=%async_computation.2 | async-start | bytes 393216 | tf_op jit(solution)/shard_map/psum | solution.py:42
  259.5 215.3 %copy-start.2 = (f32[6,1536]{1,0:T(8,128)S(1)}, f32[6,1536]{1,0:T(8,128)}, u32[]{:S(2)}) copy-start(f32[6,1536]{1,0:T(8,128)} %param.13) | copy-start | bytes 110596
  259.5 215.2 %copy-start.3 = (f32[6,1536]{1,0:T(8,128)S(1)}, f32[6,1536]{1,0:T(8,128)}, u32[]{:S(2)}) copy-start(f32[6,1536]{1,0:T(8,128)} %param.14) | copy-start | bytes 110596
  259.5 217.2 %copy-start.7 = (u32[256]{0:T(256)S(1)}, u32[256]{0:T(256)}, u32[]{:S(2)}) copy-start(u32[256]{0:T(256)} %constant.38) | copy-start | bytes 3076
  259.5 218.4 %copy-start.4 = (bf16[1,5376]{1,0:T(2,128)(2,1)S(1)}, bf16[1,5376]{1,0:T(2,128)(2,1)}, u32[]{:S(2)}) copy-start(bf16[1,5376]{1,0:T(2,128)(2,1)} %param.15) | copy-start | bytes 32260
  259.5 904.8 %copy-start.5 = (f32[42]{0:T(128)S(1)}, f32[42]{0:T(128)}, u32[]{:S(2)}) copy-start(f32[42]{0:T(128)} %param.16) | copy-start | bytes 508
  259.5 904.8 %copy-start.6 = (f32[42]{0:T(128)S(1)}, f32[42]{0:T(128)}, u32[]{:S(2)}) copy-start(f32[42]{0:T(128)} %param.17) | copy-start | bytes 508
  262.7 1590.8 %all-gather.3.cloned.1.call-start = ((), (), s32[]{:S(2)}) async-start(), calls=%async_computation.3 | async-start | bytes 3170304 | tf_op jit(solution)/shard_map/all_gather | solution.py:53
Sparse Core Ops, SparseCore 0:
  11.3 30.0 all-reduce.4
  46.9 211.2 all-reduce.6
  265.2 209.4 all-reduce.8
  478.8 112.9 all-gather.2
